TPU v7x, 32 devices: a whole 2x2x4 slice. The times are simulated.
32 devices in a mesh: dp: 8 (over z, core), ctx: 4 (over y, x).
Axes of the slice: x: 2, y: 2, z: 4, core: 2. Of those that a mesh axis runs over, the one named last changes fastest.
Arguments:
- hidden_in: bfloat16 [8, 2048, 2048], P('dp', 'ctx'), may hold values from -6 to 6
- ln_gain: bfloat16 [2048], P(('dp', 'ctx')), may hold values from 0.099609375 to 1.8984375
- ln_bias: bfloat16 [2048], P(('dp', 'ctx')), may hold values from -4 to 4
- w_qkv: bfloat16 [2048, 6144], P(('dp', 'ctx')), may hold values from -0.125 to 0.125
- b_qkv: bfloat16 [6144], P(('dp', 'ctx')), may hold values from -4 to 4
- w_out: bfloat16 [2048, 2048], P(('dp', 'ctx')), may hold values from -2 to 2
- b_out: bfloat16 [2048], P(('dp', 'ctx')), may hold values from -4 to 4
- w_up: bfloat16 [2048, 8192], P(('dp', 'ctx')), may hold values from -0.125 to 0.125
- b_up: bfloat16 [8192], P(('dp', 'ctx')), may hold values from -4 to 4
- w_down: bfloat16 [8192, 2048], P(('dp', 'ctx')), may hold values from -0.0625 to 0.0625
- b_down: bfloat16 [2048], P(('dp', 'ctx')), may hold values from -4 to 4
- segment_ids: int32 [8, 2048], P('dp'), may hold values from 0 to 3, as said below
- positions: int32 [8, 2048], P('dp', 'ctx'), may hold values from 0 to 1023, as said below
- token_order: int32 [8, 2048], P('dp'), may hold values from 0 to 2047, as said below
- grad_out: bfloat16 [8, 2048, 2048], P('dp', 'ctx'), may hold values from -6 to 6
Outputs:
- output: bfloat16 [8, 2048, 2048], P('dp', 'ctx')
- grad_in: bfloat16 [8, 2048, 2048], P('dp', 'ctx')
- grad_ln_gain: float32 [2048], P(('dp', 'ctx'))
- grad_ln_bias: float32 [2048], P(('dp', 'ctx'))
- grad_w_qkv: float32 [2048, 6144], P(('dp', 'ctx'))
- grad_b_qkv: float32 [6144], P(('dp', 'ctx'))
- grad_w_out: float32 [2048, 2048], P(('dp', 'ctx'))
- grad_b_out: float32 [2048], P(('dp', 'ctx'))
- grad_w_up: float32 [2048, 8192], P(('dp', 'ctx'))
- grad_b_up: float32 [8192], P(('dp', 'ctx'))
- grad_w_down: float32 [8192, 2048], P(('dp', 'ctx'))
- grad_b_down: float32 [2048], P(('dp', 'ctx'))
Inputs may be any that keep to these rules, and one draw needn't show every extreme that they name: Each row's places 0 to 2047 form 4 documents of consecutive places, numbered in order of place, one of which holds exactly 1024 places; segment_ids gives the document of the place token_order assigns to each slot. `positions`: A slot's place minus the first place of its document. `token_order`: each row is a permutation of its places that moves whole runs of 128 places: slots 128 b to 128 b + 127 hold the places of one run in rising order.
All inputs are finite; a program needn't handle non-finite values.
Results may differ from a plain program's by a relative error of at most 0.0095.
Values may be sent and summed in bfloat16 or wider, within the bound.
No kernel may reach another device: no remote copies, remote signals or barrier semaphores. Data moves between devices by JAX's collectives and lax.ppermute only.
A program may use at most 512 MiB of HBM per device.

v0:
```python
import math
import jax
import jax.numpy as jnp
from jax import lax
from jax.sharding import PartitionSpec as P

HEAD = 64
ROT = 32
EPS = 1e-05
NEG = -1e30


def norm_rows(values, gain, shift):
    average = jnp.mean(values, axis=-1, keepdims=True)
    centred = values - average
    variance = jnp.mean(centred * centred, axis=-1, keepdims=True)
    return centred * lax.rsqrt(variance + EPS) * gain + shift


def angle_table(position_rows):
    half_width = ROT // 2
    frequency = 10000.0 ** (-jnp.arange(half_width, dtype=jnp.float32) * 2.0 / ROT)
    angles = position_rows.astype(jnp.float32)[..., None] * frequency
    return (jnp.cos(angles)[..., None, :], jnp.sin(angles)[..., None, :])


def rotate(values, cosine, sine_table):
    half_width = cosine.shape[-1]
    front_part = values[..., :half_width]
    back_part = values[..., half_width : 2 * half_width]
    return jnp.concatenate(
        [
            front_part * cosine - back_part * sine_table,
            back_part * cosine + front_part * sine_table,
            values[..., 2 * half_width :],
        ],
        axis=-1,
    )


def unrotate(gradient, cosine, sine_table):
    half_width = cosine.shape[-1]
    front_part = gradient[..., :half_width]
    back_part = gradient[..., half_width : 2 * half_width]
    return jnp.concatenate(
        [
            front_part * cosine + back_part * sine_table,
            back_part * cosine - front_part * sine_table,
            gradient[..., 2 * half_width :],
        ],
        axis=-1,
    )


def head_groups(tensor, group_size):
    row_count, slot_count, head_count, head_width = tensor.shape
    shaped = tensor.reshape(row_count, slot_count, head_count // group_size, group_size, head_width)
    return jnp.moveaxis(shaped, 2, 0)


def join_groups(tensor):
    group_count, row_count, slot_count, group_size, head_width = tensor.shape
    return jnp.moveaxis(tensor, 0, 2).reshape(
        row_count, slot_count, group_count * group_size, head_width
    )


def masked_scores(q_group, k_group, allowed, score_scale):
    scores = (
        jnp.einsum("btge,blge->bgtl", q_group, k_group, preferred_element_type=jnp.float32)
        * score_scale
    )
    return jnp.where(allowed[:, None], scores, NEG)


def attend(queries, keys_all, values_all, allowed, score_scale):

    def one_group(pieces):
        q_group, k_group, v_group = pieces
        scores = masked_scores(q_group, k_group, allowed, score_scale)
        row_top = jnp.max(scores, axis=-1, keepdims=True)
        weights = jnp.exp(scores - row_top)
        totals = jnp.sum(weights, axis=-1, keepdims=True)
        probabilities = (weights / totals).astype(jnp.bfloat16)
        mixed_out = jnp.einsum(
            "bgtl,blge->btge", probabilities, v_group, preferred_element_type=jnp.float32
        )
        return (mixed_out.astype(jnp.bfloat16), (row_top + jnp.log(totals))[..., 0])

    return lax.map(one_group, (queries, keys_all, values_all))


def attend_back(queries, keys_all, values_all, d_attended, log_totals, allowed, score_scale):

    def one_group(pieces):
        q_group, k_group, v_group, d_group, l_group = pieces
        scores = masked_scores(q_group, k_group, allowed, score_scale)
        probs_full = jnp.exp(scores - l_group[..., None])
        probs_low = probs_full.astype(jnp.bfloat16)
        d_probs = jnp.einsum(
            "btge,blge->bgtl", d_group, v_group, preferred_element_type=jnp.float32
        )
        inner_sum = jnp.sum(probs_full * d_probs, axis=-1, keepdims=True)
        d_scores = (probs_full * (d_probs - inner_sum)).astype(jnp.bfloat16)
        d_query = (
            jnp.einsum("bgtl,blge->btge", d_scores, k_group, preferred_element_type=jnp.float32)
            * score_scale
        )
        d_key = (
            jnp.einsum("bgtl,btge->blge", d_scores, q_group, preferred_element_type=jnp.float32)
            * score_scale
        )
        d_value = jnp.einsum(
            "bgtl,btge->blge", probs_low, d_group, preferred_element_type=jnp.float32
        )
        return (d_query, d_key, d_value)

    return lax.map(one_group, (queries, keys_all, values_all, d_attended, log_totals))


def run_forward(weights, hidden_in, positions, segment_ids, token_order, fetch):
    w_qkv, w_out, w_up, w_down, b_qkv, b_out, b_up, b_down, ln_gain, ln_bias = weights
    row_count, slot_count, feature = hidden_in.shape
    head_count = feature // HEAD
    group_size = math.gcd(head_count, 4)
    hidden_f = hidden_in.astype(jnp.float32)
    normed = norm_rows(hidden_f, ln_gain.astype(jnp.float32), ln_bias.astype(jnp.float32)).astype(
        jnp.bfloat16
    )
    qkv = jnp.einsum(
        "btd,df->btf", normed, w_qkv, preferred_element_type=jnp.float32
    ) + b_qkv.astype(jnp.float32)
    cosine, sine_table = angle_table(positions)
    queries = rotate(
        qkv[..., :feature].reshape(row_count, slot_count, head_count, HEAD), cosine, sine_table
    ).astype(jnp.bfloat16)
    keys_local = rotate(
        qkv[..., feature : 2 * feature].reshape(row_count, slot_count, head_count, HEAD),
        cosine,
        sine_table,
    ).astype(jnp.bfloat16)
    values_local = qkv[..., 2 * feature :].astype(jnp.bfloat16)
    keys_all, values_all = fetch(keys_local.reshape(row_count, slot_count, feature), values_local)
    slot_start = lax.axis_index("ctx") * slot_count
    segment_local = lax.dynamic_slice_in_dim(segment_ids, slot_start, slot_count, 1)
    order_local = lax.dynamic_slice_in_dim(token_order, slot_start, slot_count, 1)
    allowed = (segment_local[:, :, None] == segment_ids[:, None, :]) & (
        token_order[:, None, :] <= order_local[:, :, None]
    )
    keys_heads = keys_all.reshape(row_count, -1, head_count, HEAD)
    values_heads = values_all.reshape(row_count, -1, head_count, HEAD)
    mixed_out, log_totals = attend(
        head_groups(queries, group_size),
        head_groups(keys_heads, group_size),
        head_groups(values_heads, group_size),
        allowed,
        HEAD ** (-0.5),
    )
    attended = join_groups(mixed_out).reshape(row_count, slot_count, feature)
    attn_out = jnp.einsum(
        "btd,de->bte", attended, w_out, preferred_element_type=jnp.float32
    ) + b_out.astype(jnp.float32)
    up_proj = jnp.einsum(
        "btd,df->btf", normed, w_up, preferred_element_type=jnp.float32
    ) + b_up.astype(jnp.float32)
    active = jax.nn.gelu(up_proj, approximate=True).astype(jnp.bfloat16)
    mlp_out = jnp.einsum(
        "btf,fd->btd", active, w_down, preferred_element_type=jnp.float32
    ) + b_down.astype(jnp.float32)
    output = (hidden_f + attn_out + mlp_out).astype(jnp.bfloat16)
    return (
        hidden_f,
        normed,
        queries,
        keys_heads,
        values_heads,
        allowed,
        attended,
        log_totals,
        up_proj,
        active,
        output,
        cosine,
        sine_table,
        group_size,
    )


def outer_rows(left, right):

    def term(start, count):
        return jnp.einsum("btd,btf->df", left, right, preferred_element_type=jnp.float32)

    return term


def reduce_rows(term, own_rows):
    return lax.psum_scatter(
        term(jnp.int32(0), own_rows * lax.axis_size(("dp", "ctx"))),
        ("dp", "ctx"),
        scatter_dimension=0,
        tiled=True,
    )


def on_device(
    hidden_in,
    ln_gain,
    ln_bias,
    w_qkv,
    b_qkv,
    w_out,
    b_out,
    w_up,
    b_up,
    w_down,
    b_down,
    segment_ids,
    positions,
    token_order,
    grad_out,
):
    weights = (
        lax.all_gather(w_qkv, ("dp", "ctx"), axis=0, tiled=True),
        lax.all_gather(w_out, ("dp", "ctx"), axis=0, tiled=True),
        lax.all_gather(w_up, ("dp", "ctx"), axis=0, tiled=True),
        lax.all_gather(w_down, ("dp", "ctx"), axis=0, tiled=True),
        lax.all_gather(b_qkv, ("dp", "ctx"), axis=0, tiled=True),
        lax.all_gather(b_out, ("dp", "ctx"), axis=0, tiled=True),
        lax.all_gather(b_up, ("dp", "ctx"), axis=0, tiled=True),
        lax.all_gather(b_down, ("dp", "ctx"), axis=0, tiled=True),
        lax.all_gather(ln_gain, ("dp", "ctx"), axis=0, tiled=True),
        lax.all_gather(ln_bias, ("dp", "ctx"), axis=0, tiled=True),
    )

    def fetch_first(keys_local, values_local):
        return (
            lax.all_gather(keys_local, "ctx", axis=1, tiled=True),
            lax.all_gather(values_local, "ctx", axis=1, tiled=True),
        )

    state = run_forward(weights, hidden_in, positions, segment_ids, token_order, fetch_first)
    output = state[10]
    weights = (
        lax.all_gather(w_qkv, ("dp", "ctx"), axis=0, tiled=True),
        lax.all_gather(w_out, ("dp", "ctx"), axis=0, tiled=True),
        lax.all_gather(w_up, ("dp", "ctx"), axis=0, tiled=True),
        lax.all_gather(w_down, ("dp", "ctx"), axis=0, tiled=True),
        lax.all_gather(b_qkv, ("dp", "ctx"), axis=0, tiled=True),
        lax.all_gather(b_out, ("dp", "ctx"), axis=0, tiled=True),
        lax.all_gather(b_up, ("dp", "ctx"), axis=0, tiled=True),
        lax.all_gather(b_down, ("dp", "ctx"), axis=0, tiled=True),
        lax.all_gather(ln_gain, ("dp", "ctx"), axis=0, tiled=True),
        lax.all_gather(ln_bias, ("dp", "ctx"), axis=0, tiled=True),
    )

    def fetch_again(keys_local, values_local):
        return (
            lax.all_gather(keys_local, "ctx", axis=1, tiled=True),
            lax.all_gather(values_local, "ctx", axis=1, tiled=True),
        )

    state = run_forward(weights, hidden_in, positions, segment_ids, token_order, fetch_again)
    hidden_f, normed, queries, keys_heads, values_heads, allowed = (
        state[0],
        state[1],
        state[2],
        state[3],
        state[4],
        state[5],
    )
    attended, log_totals, up_proj, active = (state[6], state[7], state[8], state[9])
    cosine, sine_table, group_size = (state[11], state[12], state[13])
    w_qkv_all, w_out_all, w_up_all, w_down_all = (weights[0], weights[1], weights[2], weights[3])
    gain_all = weights[8].astype(jnp.float32)
    shift_all = weights[9].astype(jnp.float32)
    row_count, slot_count, feature = hidden_in.shape
    head_count = feature // HEAD
    grad_f = grad_out.astype(jnp.float32)
    bias_grad = jnp.sum(grad_f, axis=(0, 1))
    down_grad = reduce_rows(outer_rows(active, grad_out), w_down.shape[0])
    d_active = jnp.einsum("btd,fd->btf", grad_out, w_down_all, preferred_element_type=jnp.float32)
    gelu_back = jax.vjp(lambda pre_act: jax.nn.gelu(pre_act, approximate=True), up_proj)[1]
    d_up = gelu_back(d_active)[0].astype(jnp.bfloat16)
    up_bias_grad = jnp.sum(d_up.astype(jnp.float32), axis=(0, 1))
    up_grad = reduce_rows(outer_rows(normed, d_up), w_up.shape[0])
    d_normed = jnp.einsum("btf,df->btd", d_up, w_up_all, preferred_element_type=jnp.float32)
    out_grad = reduce_rows(outer_rows(attended, grad_out), w_out.shape[0])
    d_attended = jnp.einsum(
        "bte,de->btd", grad_out, w_out_all, preferred_element_type=jnp.float32
    ).astype(jnp.bfloat16)
    d_groups = head_groups(d_attended.reshape(row_count, slot_count, head_count, HEAD), group_size)
    d_query, d_key, d_value = attend_back(
        head_groups(queries, group_size),
        head_groups(keys_heads, group_size),
        head_groups(values_heads, group_size),
        d_groups,
        log_totals,
        allowed,
        HEAD ** (-0.5),
    )
    d_query = join_groups(d_query)
    d_key_all = join_groups(d_key).reshape(row_count, -1, feature)
    d_value_all = join_groups(d_value).reshape(row_count, -1, feature)
    d_key_own, d_value_own = (
        lax.psum_scatter(d_key_all, "ctx", scatter_dimension=1, tiled=True),
        lax.psum_scatter(d_value_all, "ctx", scatter_dimension=1, tiled=True),
    )
    d_qkv = jnp.concatenate(
        [
            unrotate(d_query, cosine, sine_table).reshape(row_count, slot_count, feature),
            unrotate(
                d_key_own.reshape(row_count, slot_count, head_count, HEAD), cosine, sine_table
            ).reshape(row_count, slot_count, feature),
            d_value_own,
        ],
        axis=-1,
    ).astype(jnp.bfloat16)
    qkv_bias_grad = jnp.sum(d_qkv.astype(jnp.float32), axis=(0, 1))
    qkv_grad = reduce_rows(outer_rows(normed, d_qkv), w_qkv.shape[0])
    d_normed = d_normed + jnp.einsum(
        "btf,df->btd", d_qkv, w_qkv_all, preferred_element_type=jnp.float32
    )
    norm_back = jax.vjp(norm_rows, hidden_f, gain_all, shift_all)[1]
    d_hidden, gain_grad, shift_grad = norm_back(d_normed)
    grad_in = (grad_f + d_hidden).astype(jnp.bfloat16)
    small = (
        lax.psum_scatter(qkv_bias_grad, ("dp", "ctx"), scatter_dimension=0, tiled=True),
        lax.psum_scatter(bias_grad, ("dp", "ctx"), scatter_dimension=0, tiled=True),
        lax.psum_scatter(up_bias_grad, ("dp", "ctx"), scatter_dimension=0, tiled=True),
        lax.psum_scatter(gain_grad, ("dp", "ctx"), scatter_dimension=0, tiled=True),
        lax.psum_scatter(shift_grad, ("dp", "ctx"), scatter_dimension=0, tiled=True),
    )
    return (
        output,
        grad_in,
        small[3],
        small[4],
        qkv_grad,
        small[0],
        out_grad,
        small[1],
        up_grad,
        small[2],
        down_grad,
        small[1],
    )


def solution(mesh):
    in_specs = (
        P("dp", "ctx", None),
        P(("dp", "ctx")),
        P(("dp", "ctx")),
        P(("dp", "ctx"), None),
        P(("dp", "ctx")),
        P(("dp", "ctx"), None),
        P(("dp", "ctx")),
        P(("dp", "ctx"), None),
        P(("dp", "ctx")),
        P(("dp", "ctx"), None),
        P(("dp", "ctx")),
        P("dp", None),
        P("dp", "ctx"),
        P("dp", None),
        P("dp", "ctx", None),
    )
    out_specs = (
        P("dp", "ctx", None),
        P("dp", "ctx", None),
        P(("dp", "ctx")),
        P(("dp", "ctx")),
        P(("dp", "ctx"), None),
        P(("dp", "ctx")),
        P(("dp", "ctx"), None),
        P(("dp", "ctx")),
        P(("dp", "ctx"), None),
        P(("dp", "ctx")),
        P(("dp", "ctx"), None),
        P(("dp", "ctx")),
    )
    return jax.shard_map(
        on_device, mesh=mesh, in_specs=in_specs, out_specs=out_specs, check_vma=False
    )
```

profile of v0, /device:TPU:0, one launch (start us, length us, event | category | flops | bytes accessed | tf_op | source)
XLA Modules:
  0.0 5165.6 jit_solution(12216584643388351475)
XLA Ops:
  13.0 44.1 all-reduce.11
  60.4 109.6 %all-gather.8.cloned.1.call-done = bf16[2048,6144]{1,0:T(8,128)(2,1)} async-done(((bf16[64,6144]{1,0:T(8,128)(2,1)}), bf16[2048,6144]{1,0:T(8,128)(2,1)}) %all-gather.8.cloned.1.call-update) | async-done | bytes 25165840 | tf_op jit(solution)/shard_map/all_gather | solution.py:224
  170.0 20.8 add_bitcast_fusion
  221.4 27.3 all-gather.14.cloned.1.call-done
  262.0 75.2 %all-gather.10.cloned.1.call-done = bf16[1,2048,2048]{2,1,0:T(8,128)(2,1)} async-done(((bf16[1,512,2048]{2,1,0:T(8,128)(2,1)}), bf16[1,2048,2048]{2,1,0:T(8,128)(2,1)}) %all-gather.10.cloned.1.call-update) | async-done | bytes 8388624 | tf_op jit(solution)/shard_map/all_gather | solution.py:239
  337.3 12.4 copy.52
  349.7 77.3 %all-gather.12.cloned.1.call-done = bf16[1,2048,2048]{1,2,0:T(8,128)(2,1)} async-done(((bf16[1,512,2048]{1,2,0:T(8,128)(2,1)}), bf16[1,2048,2048]{1,2,0:T(8,128)(2,1)}) %all-gather.12.cloned.1.call-update) | async-done | bytes 8388624 | tf_op jit(solution)/shard_map/all_gather | solution.py:238
  428.6 134.3 %while.40 = (s32[]{:T(128)}, bf16[8,1,512,4,64]{2,4,3,1,0:T(8,128)(2,1)}, f32[8,1,4,512]{3,2,1,0:T(4,128)S(1)}, bf16[8,1,2048,4,64]{2,4,3,1,0:T(8,128)(2,1)}, bf...) while((s32[]{:T(128)}, ...), condition=%wide.region_9.10_spmd.clone, body=%wide.region_6.9_spmd.clone.sunk | while | flops 1127348224 | bytes 57235568 | solution.py:90
  562.9 488.6 %while.41 = (s32[]{:T(128)}, f32[8,1,512,4,64]{2,4,3,1,0:T(8,128)}, f32[8,1,2048,4,64]{2,4,3,1,0:T(8,128)}, f32[8,1,2048,4,64]{2,4,3,1,0:T(8,128)}, bf16[8,1,204...) while((s32[]{:T(128)}, f32[8,1,512,4,64]{2,4,3,1,0:T(8,128)}, ...), condition=%wide.region_12.13_spmd.clone, body=%wide.region_10.12_spmd.clone.sunk | while | flops 2751068160 | bytes 189351168 | solution.py:118
  563.3 9.4 fusion.205
  573.5 12.9 multiply_reduce_fusion.2
  586.5 16.8 multiply_convert_fusion.5
  624.6 9.8 fusion.205
  635.3 13.1 multiply_reduce_fusion.2
  648.4 16.0 multiply_convert_fusion.5
  686.4 9.4 fusion.205
  696.7 13.0 multiply_reduce_fusion.2
  709.7 17.9 multiply_convert_fusion.5
  750.0 9.4 fusion.205
  760.3 12.8 multiply_reduce_fusion.2
  773.1 17.3 multiply_convert_fusion.5
  811.3 9.7 fusion.205
  821.8 12.8 multiply_reduce_fusion.2
  834.7 15.8 multiply_convert_fusion.5
  871.5 9.4 fusion.205
  881.8 12.8 multiply_reduce_fusion.2
  894.6 15.8 multiply_convert_fusion.5
  931.4 9.4 fusion.205
  941.7 12.8 multiply_reduce_fusion.2
  954.5 15.8 multiply_convert_fusion.5
  991.3 9.4 fusion.205
  1001.6 12.8 multiply_reduce_fusion.2
  1014.5 15.8 multiply_convert_fusion.5
  1053.6 69.4 %all-gather = bf16[32,1,256]{2,1,0:T(2,128)(2,1)S(1)} all-gather(bf16[1,1,256]{2,1,0:T(2,128)(2,1)S(1)} %reshape.719), channel_id=1, replica_groups=mesh['dp'=8,'ctx'=4] {'dp','ctx'}, dimensions={0}, use_global_device_ids=true | all-gather | bytes 16896 | tf_op jit(solution)/shard_map/all_gather | solution.py:230
  1125.1 27.6 fusion.138
  1152.7 34.9 convert_reduce_fusion
  1187.6 25.5 fusion.152
  1220.8 144.8 %reduce-scatter.9.cloned.1.call-done = f32[1,512,2048]{1,2,0:T(8,128)} async-done(((f32[1,2048,2048]{1,2,0:T(8,128)}), f32[1,512,2048]{1,2,0:T(8,128)}) %reduce-scatter.9.cloned.1.call-update) | async-done | bytes 4194320 | tf_op jit(solution)/shard_map/reduce_scatter | solution.py:307
  1369.4 26.0 fusion.117
  1410.5 9.6 convert_reduce_fusion.1
  1420.2 12.5 fusion.124
  1433.4 23.9 fusion.120
  1457.4 29.6 fusion.135
  1488.6 32.4 fusion.122
  1522.0 162.6 %while.39 = (s32[]{:T(128)}, bf16[8,1,512,4,64]{2,4,3,1,0:T(8,128)(2,1)S(1)}, bf16[8,1,2048,4,64]{2,4,3,1,0:T(8,128)(2,1)}, bf16[8,1,512,4,64]{2,4,3,1,0:T(8,128...) while((s32[]{:T(128)}, ...), condition=%wide.region_5.6_spmd.clone, body=%wide.region_2.5_spmd.clone.sunk | while | flops 1102186496 | bytes 38312036 | solution.py:90
  1523.0 10.5 fusion.191
  1543.2 10.5 fusion.191
  1563.4 10.5 fusion.191
  1573.9 8.9 fusion.192
  1583.8 10.5 fusion.191
  1594.3 8.9 fusion.192
  1604.2 10.5 fusion.191
  1614.6 8.9 fusion.192
  1624.5 10.5 fusion.191
  1635.0 8.9 fusion.192
  1644.8 10.5 fusion.191
  1655.3 8.9 fusion.192
  1665.2 10.5 fusion.191
  1675.7 8.9 fusion.192
  1692.0 26.9 fusion.119
  1724.9 179.5 %reduce-scatter.13.cloned.1.call-done = f32[64,2048]{1,0:T(8,128)} async-done(((f32[2048,2048]{1,0:T(8,128)}), f32[64,2048]{1,0:T(8,128)}) %reduce-scatter.13.cloned.1.call-update) | async-done | bytes 524304 | tf_op jit(solution)/shard_map/reduce_scatter | solution.py:198
  1904.3 440.1 %reduce-scatter.11.cloned.1.call-done = f32[64,6144]{1,0:T(8,128)} async-done(((f32[2048,6144]{1,0:T(8,128)}), f32[64,6144]{1,0:T(8,128)}) %reduce-scatter.11.cloned.1.call-update) | async-done | bytes 1572880 | tf_op jit(solution)/shard_map/reduce_scatter | solution.py:198
  2344.5 1406.1 %reduce-scatter.15.cloned.1.call-done = f32[64,8192]{1,0:T(8,128)} async-done(((f32[2048,8192]{1,0:T(8,128)}), f32[64,8192]{1,0:T(8,128)}) %reduce-scatter.15.cloned.1.call-update) | async-done | bytes 2097168 | tf_op jit(solution)/shard_map/reduce_scatter | solution.py:198
  3750.6 1407.5 %reduce-scatter.17.cloned.1.call-done = f32[256,2048]{1,0:T(8,128)} async-done(((f32[8192,2048]{1,0:T(8,128)}), f32[256,2048]{1,0:T(8,128)}) %reduce-scatter.17.cloned.1.call-update) | async-done | bytes 2097168 | tf_op jit(solution)/shard_map/reduce_scatter | solution.py:198
  (337 shorter events, 438.5 us)
Async XLA Ops:
  7.2 51.9 %copy-start = (bf16[1,512,2048]{2,1,0:T(8,128)(2,1)S(1)}, bf16[1,512,2048]{2,1,0:T(8,128)(2,1)}, u32[]{:S(2)}) copy-start(bf16[1,512,2048]{2,1,0:T(8,128)(2,1)} %param.21) | copy-start | bytes 6291460
  7.2 162.8 %all-gather.8.cloned.1.call-start = ((), (), s32[]{:S(2)}) async-start(), calls=%async_computation.6 | async-start | bytes 25952256 | tf_op jit(solution)/shard_map/all_gather | solution.py:224
  7.9 240.7 %all-gather.14.cloned.1.call-start = ((), (), s32[]{:S(2)}) async-start(), calls=%async_computation.9 | async-start | bytes 8650752 | tf_op jit(solution)/shard_map/all_gather | solution.py:225
  8.7 328.6 %all-gather.10.cloned.1.call-start = ((), (), s32[]{:S(2)}) async-start(), calls=%async_computation.7 | async-start | bytes 10485760 | tf_op jit(solution)/shard_map/all_gather | solution.py:239
  57.1 133.7 %copy-start.15 = (f32[2048]{0:T(1024)}, f32[2048]{0:T(1024)S(1)}, u32[]{:S(2)}) copy-start(f32[2048]{0:T(1024)S(1)} %convert_element_type.146) | copy-start | bytes 24580
  57.1 133.7 %copy-start.21 = (f32[2048]{0:T(1024)}, f32[2048]{0:T(1024)S(1)}, u32[]{:S(2)}) copy-start(f32[2048]{0:T(1024)S(1)} %convert_element_type.147) | copy-start | bytes 24580
  59.1 131.7 %copy-start.17 = (f32[512]{0:T(512)}, f32[512]{0:T(512)S(1)}, u32[]{:S(2)}) copy-start(f32[512]{0:T(512)S(1)} %broadcast_multiply_fusion) | copy-start | bytes 6148
  60.4 130.4 %copy-start.19 = (f32[512]{0:T(512)}, f32[512]{0:T(512)S(1)}, u32[]{:S(2)}) copy-start(f32[512]{0:T(512)S(1)} %fusion.131) | copy-start | bytes 6148
  194.7 232.4 %all-gather.12.cloned.1.call-start = ((), (), s32[]{:S(2)}) async-start(), calls=%async_computation.8 | async-start | bytes 10485760 | tf_op jit(solution)/shard_map/all_gather | solution.py:238
  195.0 20.5 copy-start.28
  195.0 20.5 copy-start.30
  219.9 905.2 %all-gather.16.cloned.1.call-start = ((), (), s32[]{:S(2)}) async-start(), calls=%async_computation.10 | async-start | bytes 34603008 | tf_op jit(solution)/shard_map/all_gather | solution.py:226
  220.5 932.2 %all-gather.18.cloned.1.call-start = ((), (), s32[]{:S(2)}) async-start(), calls=%async_computation.11 | async-start | bytes 34603008 | tf_op jit(solution)/shard_map/all_gather | solution.py:227
  221.1 992.1 %reduce-scatter.7.cloned.1.call-start = ((), (), s32[]{:S(2)}) async-start(), calls=%async_computation.12 | async-start | bytes 20971520 | tf_op jit(solution)/shard_map/reduce_scatter | solution.py:306
  586.4 31.1 slice-start
  586.4 31.1 slice-start.1
  586.4 31.1 slice-start.2
  603.3 14.3 slice-start.3
  648.4 30.9 slice-start
  648.4 30.9 slice-start.1
  648.4 30.9 slice-start.2
  664.4 14.9 slice-start.3
  709.7 33.2 slice-start
  709.7 33.2 slice-start.1
  709.7 33.2 slice-start.2
  727.6 15.3 slice-start.3
  773.1 31.1 slice-start
  773.1 31.1 slice-start.1
  773.1 31.1 slice-start.2
  790.4 13.8 slice-start.3
  834.7 29.8 slice-start
  834.7 29.8 slice-start.1
  834.7 29.8 slice-start.2
  850.5 13.9 slice-start.3
  894.6 29.8 slice-start
  894.6 29.8 slice-start.1
  894.6 29.8 slice-start.2
  910.5 13.9 slice-start.3
  954.5 29.8 slice-start
  954.5 29.8 slice-start.1
  954.5 29.8 slice-start.2
  970.4 13.9 slice-start.3
  1014.4 29.8 slice-start
  1014.4 29.8 slice-start.1
  1014.4 29.8 slice-start.2
  1030.3 13.9 slice-start.3
  1052.8 312.8 %reduce-scatter.9.cloned.1.call-start = ((), (), s32[]{:S(2)}) async-start(), calls=%async_computation.13 | async-start | bytes 20971520 | tf_op jit(solution)/shard_map/reduce_scatter | solution.py:307
  1052.9 72.2 %copy-start.1 = (bf16[1,512,2048]{2,1,0:T(8,128)(2,1)S(1)}, bf16[1,512,2048]{2,1,0:T(8,128)(2,1)}, u32[]{:S(2)}) copy-start(bf16[1,512,2048]{2,1,0:T(8,128)(2,1)} %param.21) | copy-start | bytes 6291460
  1052.9 72.2 %copy-start.16 = (f32[2048]{0:T(1024)S(1)}, f32[2048]{0:T(1024)}, u32[]{:S(2)}) copy-start(f32[2048]{0:T(1024)} %copy-done.15) | copy-start | bytes 24580
  1052.9 72.2 %copy-start.18 = (f32[512]{0:T(512)S(1)}, f32[512]{0:T(512)}, u32[]{:S(2)}) copy-start(f32[512]{0:T(512)} %copy-done.17) | copy-start | bytes 6148
  1052.9 72.2 %copy-start.20 = (f32[512]{0:T(512)S(1)}, f32[512]{0:T(512)}, u32[]{:S(2)}) copy-start(f32[512]{0:T(512)} %copy-done.19) | copy-start | bytes 6148
  1052.9 72.2 %copy-start.22 = (f32[2048]{0:T(1024)S(1)}, f32[2048]{0:T(1024)}, u32[]{:S(2)}) copy-start(f32[2048]{0:T(1024)} %copy-done.21) | copy-start | bytes 24580
  1053.6 665.4 %all-reduce.14.cloned.1.call-start = ((), (), s32[]{:S(2)}) async-start(), calls=%async_computation.18 | async-start | bytes 163840
  1123.1 29.6 copy-start.32
  1187.6 27.3 copy-start.29
  1187.6 27.3 copy-start.31
  1369.4 26.0 copy-start.36
  1420.2 484.2 %reduce-scatter.13.cloned.1.call-start = ((), (), s32[]{:S(2)}) async-start(), calls=%async_computation.15 | async-start | bytes 17301504 | tf_op jit(solution)/shard_map/reduce_scatter | solution.py:198
  1432.7 911.7 %reduce-scatter.11.cloned.1.call-start = ((), (), s32[]{:S(2)}) async-start(), calls=%async_computation.14 | async-start | bytes 51904512 | tf_op jit(solution)/shard_map/reduce_scatter | solution.py:198
  1457.4 2293.2 %reduce-scatter.15.cloned.1.call-start = ((), (), s32[]{:S(2)}) async-start(), calls=%async_computation.16 | async-start | bytes 69206016 | tf_op jit(solution)/shard_map/reduce_scatter | solution.py:198
  1487.1 3671.1 %reduce-scatter.17.cloned.1.call-start = ((), (), s32[]{:S(2)}) async-start(), calls=%async_computation.17 | async-start | bytes 69206016 | tf_op jit(solution)/shard_map/reduce_scatter | solution.py:198
  1684.6 7.4 copy-start.2
  1684.6 7.4 copy-start.34
  1719.7 3438.9 %copy-start.41 = (f32[64]{0:T(128)}, f32[64]{0:T(128)S(1)}, u32[]{:S(2)}) copy-start(f32[64]{0:T(128)S(1)} %dynamic-slice.3) | copy-start | bytes 772
  (23 other events, 41.8 us)
Sparse Core Ops, SparseCore 0:
  10.9 159.0 all-gather.7
  172.8 75.7 all-gather.13
  251.0 86.1 all-gather.9
  339.5 87.4 all-gather.11
  429.8 194.8 all-gather.15
  627.3 192.9 all-gather.17
  1051.7 157.0 reduce-scatter.6
  1211.8 153.7 reduce-scatter.8
  1420.3 122.3 all-reduce.13
  1545.4 358.9 reduce-scatter.12
  1911.3 433.0 reduce-scatter.10
  2347.2 1403.3 reduce-scatter.14
  3753.5 1404.5 reduce-scatter.16
where the time goes:
time: 5180 us; the launch traced here: 5170 us
  waiting for transfers between devices  3870 us (75%)
  matrix products  871 us (17%)
  other arithmetic  230 us (4%)
  blocking collectives  114 us (2%)
  local copies, waits for them, and re-layouts  63.4 us (1%)
    reduce_scatter x4, waiting for transfers between devices, reduce_rows(): lax.psum_scatter(term(jnp.int32(0), own_rows * lax.axis_size(('dp', 'ctx'...  3430 us
    reduce_scatter x1, waiting for transfers between devices, on_device(): lax.psum_scatter(d_value_all, 'ctx', scatter_dimension=1, tiled=True)  145 us
    convert_element_type x8, other arithmetic, one_group(): d_scores = (probs_full * (d_probs - inner_sum)).astype(jnp.bfloat16)  131 us
    dot_general x16, matrix products, one_group(): jnp.einsum('bgtl,blge->btge', probabilities, v_group, preferred_element_t...  127 us
    dot_general x16, matrix products, masked_scores(): jnp.einsum('btge,blge->bgtl', q_group, k_group, preferred_element_type=jn...  111 us
    all_gather x1, waiting for transfers between devices, on_device(): lax.all_gather(w_qkv, ('dp', 'ctx'), axis=0, tiled=True)  110 us
  transfers between devices with their start and end apart: 13, of which 9 were waited for; matrix products, arithmetic and copies ran while one was open for 21% of the time, Pallas kernels for 0%

commit v1 on v0

--- a/solution.py
+++ b/solution.py
@@ -8,6 +8,18 @@
 ROT = 32
 EPS = 1e-05
 NEG = -1e30
+
+
+def collect(x, axis, dim):
+    ways, here, hop = (lax.axis_size(axis), lax.axis_index(axis), x.shape[dim])
+    line, have = (x, 1)
+    while have < ways:
+        line = jnp.concatenate(
+            [line, lax.ppermute(line, axis, [(d, (d - have) % ways) for d in range(ways)])],
+            axis=dim,
+        )
+        have = 2 * have
+    return jnp.roll(line, here * hop, axis=dim)
 
 
 def norm_rows(values, gain, shift):
@@ -221,7 +233,7 @@
     grad_out,
 ):
     weights = (
-        lax.all_gather(w_qkv, ("dp", "ctx"), axis=0, tiled=True),
+        collect(w_qkv, ("dp", "ctx"), 0),
         lax.all_gather(w_out, ("dp", "ctx"), axis=0, tiled=True),
         lax.all_gather(w_up, ("dp", "ctx"), axis=0, tiled=True),
         lax.all_gather(w_down, ("dp", "ctx"), axis=0, tiled=True),

time: 5180 us -> 6020 us (1.16)
  blocking collectives: 114 us -> 638 us
  waiting for transfers between devices: 3870 us -> 4050 us
  local copies, waits for them, and re-layouts: 63.4 us -> 149 us
    unnamed x1, blocking collectives: 44.1 us -> 569 us
    ppermute x0 -> x5, waiting for transfers between devices: none -> 299 us  [collect(): lax.ppermute(line, axis, [(d, (d - have) % ways) for d in range(ways)])]
    all_gather x1, waiting for transfers between devices: 110 us -> 0.01 us  [on_device(): lax.all_gather(w_qkv, ('dp', 'ctx'), axis=0, tiled=True)]
    reduce_scatter x4, waiting for transfers between devices: 3430 us -> 3540 us  [reduce_rows(): lax.psum_scatter(term(jnp.int32(0), own_rows * lax.axis_size(('dp', 'ctx'...]
    all_gather x1, waiting for transfers between devices: 75.2 us -> 0.02 us  [fetch_first(): lax.all_gather(values_local, 'ctx', axis=1, tiled=True)]
    all_gather x1, waiting for transfers between devices: 77.3 us -> 6.88 us  [fetch_first(): lax.all_gather(keys_local, 'ctx', axis=1, tiled=True)]
  transfers between devices with their start and end apart: 13 -> 20, of which waited for: 9 -> 11; matrix products, arithmetic and copies ran while one was open for 21% -> 21% of each run, Pallas kernels for 0% -> 0%
where the time goes in v1:
time: 6020 us; the launch traced here: 6010 us
  waiting for transfers between devices  4050 us (67%)
  matrix products  896 us (15%)
  blocking collectives  638 us (11%)
  other arithmetic  239 us (4%)
  local copies, waits for them, and re-layouts  149 us (2%)
    reduce_scatter x4, waiting for transfers between devices, reduce_rows(): lax.psum_scatter(term(jnp.int32(0), own_rows * lax.axis_size(('dp', 'ctx'...  3540 us
    unnamed x1, blocking collectives  569 us
    ppermute x5, waiting for transfers between devices, collect(): lax.ppermute(line, axis, [(d, (d - have) % ways) for d in range(ways)])  299 us
    reduce_scatter x1, waiting for transfers between devices, on_device(): lax.psum_scatter(d_value_all, 'ctx', scatter_dimension=1, tiled=True)  141 us
    convert_element_type x8, other arithmetic, one_group(): d_scores = (probs_full * (d_probs - inner_sum)).astype(jnp.bfloat16)  131 us
    dot_general x16, matrix products, one_group(): jnp.einsum('bgtl,blge->btge', probabilities, v_group, preferred_element_t...  127 us
  transfers between devices with their start and end apart: 20, of which 11 were waited for; matrix products, arithmetic and copies ran while one was open for 21% of the time, Pallas kernels for 0%

profile of v1, /device:TPU:0, one launch (start us, length us, event | category | flops | bytes accessed | tf_op | source)
XLA Modules:
  0.0 6011.5 jit_solution(1646301598074902948)
XLA Ops:
  14.4 18.7 collective-permute-done
  36.8 38.3 collective-permute-done.1
  77.0 10.9 collective-permute-start.2
  88.0 46.1 collective-permute-done.2
  148.3 195.5 %collective-permute-done.3 = bf16[512,6144]{1,0:T(8,128)(2,1)} collective-permute-done((bf16[512,6144]{1,0:T(8,128)(2,1)}, bf16[512,6144]{1,0:T(8,128)(2,1)}, u32[]{:S(2)}, u32[]{:S(2)}) %collective-permute-start.3) | collective-permute-done | bytes 6291488 | tf_op jit(solution)/shard_map/ppermute | solution.py:18
  355.1 569.0 %all-reduce.11 = (bf16[6144]{0:T(1024)(128)(2,1)S(1)}, bf16[2048]{0:T(1024)(128)(2,1)S(1)}, bf16[2048]{0:T(1024)(128)(2,1)S(1)}, bf16[2048]{0:T(1024)(128)(2,1)}, bf16[2048]{0:T(1024)(128)(2,1)}) all-reduce(bf16[6144]{0:T(1024)(128)(2,1)S(1)} %dynamic-update-slice.2, ...), channel_id=1, replica_groups=mesh['dp'=8,'ctx'=4] {'dp','ctx'}, use_global_device_ids=true, to_apply=%add.2 | all-reduce | flops 14336 | bytes 57344
  925.8 21.2 add_bitcast_fusion
  951.6 11.2 constant_dynamic-update-slice_fusion.11
  975.0 10.8 constant_dynamic-update-slice_fusion.5
  985.9 20.9 add_bitcast_fusion.1
  1070.8 12.3 copy.78
  1083.1 58.7 all-gather.22.cloned.1.call-done
  1143.4 134.3 %while.40 = (s32[]{:T(128)}, bf16[8,1,512,4,64]{2,4,3,1,0:T(8,128)(2,1)}, f32[8,1,4,512]{3,2,1,0:T(4,128)S(1)}, bf16[8,1,2048,4,64]{2,4,3,1,0:T(8,128)(2,1)}, bf...) while((s32[]{:T(128)}, ...), condition=%wide.region_9.10_spmd.clone, body=%wide.region_6.9_spmd.clone.sunk | while | flops 1127348224 | bytes 57235568 | solution.py:102
  1277.6 489.1 %while.41 = (s32[]{:T(128)}, f32[8,1,512,4,64]{2,4,3,1,0:T(8,128)}, f32[8,1,2048,4,64]{2,4,3,1,0:T(8,128)}, f32[8,1,2048,4,64]{2,4,3,1,0:T(8,128)}, bf16[8,1,204...) while((s32[]{:T(128)}, f32[8,1,512,4,64]{2,4,3,1,0:T(8,128)}, ...), condition=%wide.region_12.13_spmd.clone, body=%wide.region_10.12_spmd.clone.sunk | while | flops 2751068160 | bytes 189351168 | solution.py:130
  1277.8 9.4 fusion.212
  1288.1 12.9 multiply_reduce_fusion.2
  1301.1 16.8 multiply_convert_fusion.5
  1339.2 9.7 fusion.212
  1349.9 13.1 multiply_reduce_fusion.2
  1363.0 15.9 multiply_convert_fusion.5
  1401.3 9.4 fusion.212
  1411.6 13.0 multiply_reduce_fusion.2
  1424.7 18.1 multiply_convert_fusion.5
  1464.8 9.4 fusion.212
  1475.2 12.9 multiply_reduce_fusion.2
  1488.1 17.3 multiply_convert_fusion.5
  1526.1 9.7 fusion.212
  1536.7 12.9 multiply_reduce_fusion.2
  1549.6 15.8 multiply_convert_fusion.5
  1586.4 9.4 fusion.212
  1596.7 12.9 multiply_reduce_fusion.2
  1609.6 15.8 multiply_convert_fusion.5
  1646.3 9.4 fusion.212
  1656.7 12.9 multiply_reduce_fusion.2
  1669.6 15.8 multiply_convert_fusion.5
  1706.3 9.4 fusion.212
  1716.6 12.9 multiply_reduce_fusion.2
  1729.5 15.8 multiply_convert_fusion.5
  1772.3 69.3 %all-gather = bf16[32,1,256]{2,1,0:T(2,128)(2,1)S(1)} all-gather(bf16[1,1,256]{2,1,0:T(2,128)(2,1)S(1)} %reshape.807), channel_id=1, replica_groups=mesh['dp'=8,'ctx'=4] {'dp','ctx'}, dimensions={0}, use_global_device_ids=true | all-gather | bytes 16896 | tf_op jit(solution)/shard_map/all_gather | solution.py:242
  1843.7 27.6 fusion.144
  1871.3 35.6 convert_reduce_fusion
  1906.9 25.3 fusion.159
  1940.1 140.7 %reduce-scatter.9.cloned.1.call-done = f32[1,512,2048]{1,2,0:T(8,128)} async-done(((f32[1,2048,2048]{1,2,0:T(8,128)}), f32[1,512,2048]{1,2,0:T(8,128)}) %reduce-scatter.9.cloned.1.call-update) | async-done | bytes 4194320 | tf_op jit(solution)/shard_map/reduce_scatter | solution.py:319
  2084.6 25.9 fusion.121
  2119.6 9.5 convert_reduce_fusion.1
  2133.7 12.5 fusion.128
  2146.9 24.1 fusion.124
  2171.1 30.9 fusion.140
  2203.7 33.0 fusion.126
  2239.2 12.5 copy.64
  2260.3 162.3 %while.39 = (s32[]{:T(128)}, bf16[8,1,512,4,64]{2,4,3,1,0:T(8,128)(2,1)S(1)}, bf16[8,1,2048,4,64]{2,4,3,1,0:T(8,128)(2,1)}, bf16[8,1,512,4,64]{2,4,3,1,0:T(8,128...) while((s32[]{:T(128)}, ...), condition=%wide.region_5.6_spmd.clone, body=%wide.region_2.5_spmd.clone.sunk | while | flops 1102186496 | bytes 38312036 | solution.py:102
  2261.3 10.5 fusion.198
  2281.6 10.5 fusion.198
  2301.8 10.5 fusion.198
  2322.1 10.5 fusion.198
  2342.4 10.5 fusion.198
  2362.6 10.5 fusion.198
  2382.8 10.5 fusion.198
  2403.3 10.5 fusion.198
  2430.0 26.9 fusion.123
  2462.9 287.7 %reduce-scatter.13.cloned.1.call-done = f32[64,2048]{1,0:T(8,128)} async-done(((f32[2048,2048]{1,0:T(8,128)}), f32[64,2048]{1,0:T(8,128)}) %reduce-scatter.13.cloned.1.call-update) | async-done | bytes 524304 | tf_op jit(solution)/shard_map/reduce_scatter | solution.py:210
  2750.6 440.1 %reduce-scatter.11.cloned.1.call-done = f32[64,6144]{1,0:T(8,128)} async-done(((f32[2048,6144]{1,0:T(8,128)}), f32[64,6144]{1,0:T(8,128)}) %reduce-scatter.11.cloned.1.call-update) | async-done | bytes 1572880 | tf_op jit(solution)/shard_map/reduce_scatter | solution.py:210
  3190.7 1406.1 %reduce-scatter.15.cloned.1.call-done = f32[64,8192]{1,0:T(8,128)} async-done(((f32[2048,8192]{1,0:T(8,128)}), f32[64,8192]{1,0:T(8,128)}) %reduce-scatter.15.cloned.1.call-update) | async-done | bytes 2097168 | tf_op jit(solution)/shard_map/reduce_scatter | solution.py:210
  4596.8 1407.4 %reduce-scatter.17.cloned.1.call-done = f32[256,2048]{1,0:T(8,128)} async-done(((f32[8192,2048]{1,0:T(8,128)}), f32[256,2048]{1,0:T(8,128)}) %reduce-scatter.17.cloned.1.call-update) | async-done | bytes 2097168 | tf_op jit(solution)/shard_map/reduce_scatter | solution.py:210
  (407 shorter events, 572.1 us)
Async XLA Ops:
  7.2 126.9 %copy-start.4 = (bf16[64,6144]{1,0:T(8,128)(2,1)S(1)}, bf16[64,6144]{1,0:T(8,128)(2,1)}, u32[]{:S(2)}) copy-start(bf16[64,6144]{1,0:T(8,128)(2,1)} %param.24) | copy-start | bytes 2359300
  7.2 918.6 %all-gather.20.cloned.1.call-start = ((), (), s32[]{:S(2)}) async-start(), calls=%async_computation.11 | async-start | bytes 25952256 | tf_op jit(solution)/shard_map/all_gather | solution.py:257
  7.9 1049.5 %all-gather.14.cloned.1.call-start = ((), (), s32[]{:S(2)}) async-start(), calls=%async_computation.8 | async-start | bytes 8650752 | tf_op jit(solution)/shard_map/all_gather | solution.py:237
  8.0 25.2 collective-permute-start
  33.1 104.6 %copy-start.10 = (bf16[64,6144]{1,0:T(8,128)(2,1)}, bf16[64,6144]{1,0:T(8,128)(2,1)S(1)}, u32[]{:S(2)}) copy-start(bf16[64,6144]{1,0:T(8,128)(2,1)S(1)} %collective-permute-done) | copy-start | bytes 2359300
  34.7 40.5 collective-permute-start.1
  75.1 69.4 %copy-start.8 = (bf16[128,6144]{1,0:T(8,128)(2,1)}, bf16[128,6144]{1,0:T(8,128)(2,1)S(1)}, u32[]{:S(2)}) copy-start(bf16[128,6144]{1,0:T(8,128)(2,1)S(1)} %collective-permute-done.1) | copy-start | bytes 4718596
  77.0 57.0 collective-permute-start.2
  137.7 206.1 %collective-permute-start.3 = (bf16[512,6144]{1,0:T(8,128)(2,1)}, bf16[512,6144]{1,0:T(8,128)(2,1)}, u32[]{:S(2)}, u32[]{:S(2)}) collective-permute-start(bf16[512,6144]{1,0:T(8,128)(2,1)} %pad_maximum_fusion), channel_id=1, source_target_pairs={{0,24},{1,25},{2,26},{3,27},{4,28},{5,29},{6,30},{7,31},{8,0},{9,1... | collective-permute-start | bytes 18874376 | tf_op jit(solution)/shard_map/ppermute | solution.py:18
  140.3 930.5 %all-gather.24.cloned.1.call-start = ((), (), s32[]{:S(2)}) async-start(), calls=%async_computation.13 | async-start | bytes 10485760 | tf_op jit(solution)/shard_map/all_gather | solution.py:272
  148.3 195.5 %copy-start.41 = (bf16[1024,6144]{1,0:T(8,128)(2,1)}, bf16[1024,6144]{1,0:T(8,128)(2,1)S(1)}, u32[]{:S(2)}) copy-start(bf16[1024,6144]{1,0:T(8,128)(2,1)S(1)} %get-tuple-element.388) | copy-start | bytes 37748740
  343.9 580.2 %copy-start = (bf16[1,512,2048]{2,1,0:T(8,128)(2,1)S(1)}, bf16[1,512,2048]{2,1,0:T(8,128)(2,1)}, u32[]{:S(2)}) copy-start(bf16[1,512,2048]{2,1,0:T(8,128)(2,1)} %param.21) | copy-start | bytes 6291460
  353.0 598.5 %collective-permute-start.4 = (bf16[1024,6144]{1,0:T(8,128)(2,1)}, bf16[1024,6144]{1,0:T(8,128)(2,1)}, u32[]{:S(2)}, u32[]{:S(2)}) collective-permute-start(bf16[1024,6144]{1,0:T(8,128)(2,1)} %get-tuple-element.374), channel_id=1, source_target_pairs={{0,16},{1,17},{2,18},{3,19},{4,20},{5,21},{6,22},{7,23},{8,24},{9,... | collective-permute-start | bytes 37748744 | tf_op jit(solution)/shard_map/ppermute | solution.py:18
  924.1 61.8 %copy-start.24 = (f32[2048]{0:T(1024)}, f32[2048]{0:T(1024)S(1)}, u32[]{:S(2)}) copy-start(f32[2048]{0:T(1024)S(1)} %convert_element_type.167) | copy-start | bytes 24580
  924.1 61.8 %copy-start.30 = (f32[2048]{0:T(1024)}, f32[2048]{0:T(1024)S(1)}, u32[]{:S(2)}) copy-start(f32[2048]{0:T(1024)S(1)} %convert_element_type.168) | copy-start | bytes 24580
  924.5 61.4 %copy-start.26 = (f32[512]{0:T(512)}, f32[512]{0:T(512)S(1)}, u32[]{:S(2)}) copy-start(f32[512]{0:T(512)S(1)} %broadcast_multiply_fusion) | copy-start | bytes 6148
  925.8 60.1 copy-start.28
  951.0 190.8 %all-gather.22.cloned.1.call-start = ((), (), s32[]{:S(2)}) async-start(), calls=%async_computation.12 | async-start | bytes 10485760 | tf_op jit(solution)/shard_map/all_gather | solution.py:271
  951.5 96.1 %copy-start.37 = (f32[512,16]{0,1:T(8,128)}, f32[512,16]{0,1:T(8,128)S(1)}, u32[]{:S(2)}) copy-start(f32[512,16]{0,1:T(8,128)S(1)} %get-tuple-element.406) | copy-start | bytes 98308
  951.5 96.1 %copy-start.39 = (f32[512,16]{0,1:T(8,128)}, f32[512,16]{0,1:T(8,128)S(1)}, u32[]{:S(2)}) copy-start(f32[512,16]{0,1:T(8,128)S(1)} %get-tuple-element.407) | copy-start | bytes 98308
  1055.7 788.0 %all-gather.16.cloned.1.call-start = ((), (), s32[]{:S(2)}) async-start(), calls=%async_computation.9 | async-start | bytes 34603008 | tf_op jit(solution)/shard_map/all_gather | solution.py:238
  1056.3 815.0 %all-gather.18.cloned.1.call-start = ((), (), s32[]{:S(2)}) async-start(), calls=%async_computation.10 | async-start | bytes 34603008 | tf_op jit(solution)/shard_map/all_gather | solution.py:239
  1056.8 875.4 %reduce-scatter.7.cloned.1.call-start = ((), (), s32[]{:S(2)}) async-start(), calls=%async_computation.14 | async-start | bytes 20971520 | tf_op jit(solution)/shard_map/reduce_scatter | solution.py:318
  1301.1 31.1 slice-start
  1301.1 31.1 slice-start.1
  1301.1 31.1 slice-start.2
  1363.0 31.0 slice-start
  1363.0 31.0 slice-start.1
  1363.0 31.0 slice-start.2
  1424.6 33.2 slice-start
  1424.6 33.2 slice-start.1
  1424.6 33.2 slice-start.2
  1488.0 31.0 slice-start
  1488.0 31.0 slice-start.1
  1488.0 31.0 slice-start.2
  1549.5 29.8 slice-start
  1549.5 29.8 slice-start.1
  1549.5 29.8 slice-start.2
  1609.5 29.8 slice-start
  1609.5 29.8 slice-start.1
  1609.5 29.8 slice-start.2
  1669.5 29.8 slice-start
  1669.5 29.8 slice-start.1
  1669.5 29.8 slice-start.2
  1729.5 29.9 slice-start
  1729.5 29.9 slice-start.1
  1729.5 29.9 slice-start.2
  1767.4 313.4 %reduce-scatter.9.cloned.1.call-start = ((), (), s32[]{:S(2)}) async-start(), calls=%async_computation.15 | async-start | bytes 20971520 | tf_op jit(solution)/shard_map/reduce_scatter | solution.py:319
  1768.1 75.5 %copy-start.1 = (bf16[1,512,2048]{2,1,0:T(8,128)(2,1)S(1)}, bf16[1,512,2048]{2,1,0:T(8,128)(2,1)}, u32[]{:S(2)}) copy-start(bf16[1,512,2048]{2,1,0:T(8,128)(2,1)} %param.21) | copy-start | bytes 6291460
  1768.2 75.5 %copy-start.25 = (f32[2048]{0:T(1024)S(1)}, f32[2048]{0:T(1024)}, u32[]{:S(2)}) copy-start(f32[2048]{0:T(1024)} %copy-done.24) | copy-start | bytes 24580
  1768.2 75.5 %copy-start.27 = (f32[512]{0:T(512)S(1)}, f32[512]{0:T(512)}, u32[]{:S(2)}) copy-start(f32[512]{0:T(512)} %copy-done.26) | copy-start | bytes 6148
  1768.2 75.5 %copy-start.29 = (f32[512]{0:T(512)S(1)}, f32[512]{0:T(512)}, u32[]{:S(2)}) copy-start(f32[512]{0:T(512)} %copy-done.28) | copy-start | bytes 6148
  1768.2 75.5 %copy-start.31 = (f32[2048]{0:T(1024)S(1)}, f32[2048]{0:T(1024)}, u32[]{:S(2)}) copy-start(f32[2048]{0:T(1024)} %copy-done.30) | copy-start | bytes 24580
  1768.2 471.0 %all-gather.10.cloned.1.call-start = ((), (), s32[]{:S(2)}) async-start(), calls=%async_computation.6 | async-start | bytes 10485760 | tf_op jit(solution)/shard_map/all_gather | solution.py:251
  1772.2 487.8 %all-gather.12.cloned.1.call-start = ((), (), s32[]{:S(2)}) async-start(), calls=%async_computation.7 | async-start | bytes 10485760 | tf_op jit(solution)/shard_map/all_gather | solution.py:250
  1841.6 29.7 copy-start.42
  1841.7 615.3 %all-reduce.14.cloned.1.call-start = ((), (), s32[]{:S(2)}) async-start(), calls=%async_computation.20 | async-start | bytes 163840
  1906.9 27.4 copy-start.38
  1906.9 27.4 copy-start.40
  2133.7 616.9 %reduce-scatter.13.cloned.1.call-start = ((), (), s32[]{:S(2)}) async-start(), calls=%async_computation.17 | async-start | bytes 17301504 | tf_op jit(solution)/shard_map/reduce_scatter | solution.py:210
  2146.3 1044.4 %reduce-scatter.11.cloned.1.call-start = ((), (), s32[]{:S(2)}) async-start(), calls=%async_computation.16 | async-start | bytes 51904512 | tf_op jit(solution)/shard_map/reduce_scatter | solution.py:210
  2171.1 2425.7 %reduce-scatter.15.cloned.1.call-start = ((), (), s32[]{:S(2)}) async-start(), calls=%async_computation.18 | async-start | bytes 69206016 | tf_op jit(solution)/shard_map/reduce_scatter | solution.py:210
  2202.1 3802.1 %reduce-scatter.17.cloned.1.call-start = ((), (), s32[]{:S(2)}) async-start(), calls=%async_computation.19 | async-start | bytes 69206016 | tf_op jit(solution)/shard_map/reduce_scatter | solution.py:210
  2457.7 3547.0 %copy-start.56 = (f32[64]{0:T(128)}, f32[64]{0:T(128)S(1)}, u32[]{:S(2)}) copy-start(f32[64]{0:T(128)S(1)} %dynamic-slice.3) | copy-start | bytes 772
  (45 other events, 336.5 us)
Sparse Core Ops, SparseCore 0:
  10.9 265.7 all-gather.19
  279.6 680.0 all-gather.13
  962.1 86.1 all-gather.23
  1055.8 85.9 all-gather.21
  1144.5 194.8 all-gather.15
  1342.1 192.9 all-gather.17
  1767.0 156.9 reduce-scatter.6
  1927.0 153.7 reduce-scatter.8
  2083.2 87.5 all-gather.9
  2172.6 87.4 all-gather.11
  2266.5 122.3 all-reduce.13
  2391.7 358.9 reduce-scatter.12
  2757.6 433.0 reduce-scatter.10
  3193.5 1403.2 reduce-scatter.14
  4599.6 1404.5 reduce-scatter.16
